TPU v7x, 32 devices: a whole 2x2x4 slice. The times are simulated.
32 devices in a mesh: pairs: 2 (over x), src: 8 (over z, y), tgt: 2 (over core).
Axes of the slice: x: 2, y: 2, z: 4, core: 2. Of those that a mesh axis runs over, the one named last changes fastest.
Arguments:
- src_feat: float32 [2048, 32], P(('pairs', 'src'), 'tgt'), parts along dimension 0, may hold values from -0.72 to 0.72
- tgt_feat: float32 [32768, 32], P(('pairs', 'tgt'), 'src'), parts along dimension 0, may hold values from -0.72 to 0.72
- tgt_dual: float32 [32768], P(('pairs', 'tgt')), parts along dimension 0, may hold values from -6 to 6
- core_matrix: float32 [68, 34], P('pairs'), parts along dimension 0, may hold values from -3 to 3
Outputs:
- src_dual: float32 [2048], P(('pairs', 'src')), parts along dimension 0
- tgt_dual_out: float32 [32768], P(('pairs', 'tgt')), parts along dimension 0
- core_out: float32 [68, 34], P('pairs'), parts along dimension 0
There are 2 independent parts, one for each index of `pairs`. A program takes and returns all parts, laid end to end along the dimension named above; each array names one. Nothing has to cross between parts.
All inputs are finite; a program needn't handle non-finite values.
Results may differ from a plain program's by a relative error of at most 0.0003.
Values sent between devices are 32-bit elements; how exact they have to be, the bound alone decides.
No kernel may reach another device: no remote copies, remote signals or barrier semaphores. Data moves between devices by JAX's collectives and lax.ppermute only.
A program may use at most 64 MiB of HBM per device.

v0:
```python
import jax
import jax.numpy as jnp
from jax import lax
from jax.sharding import PartitionSpec as P

OUTER = 2


EPSILON = 0.02
HIGH = lax.Precision.HIGHEST


def merged(array, axis, combine):
    everything = jax.tree.map(lambda part: lax.all_gather(part, axis), array)
    leading = jax.tree.map(lambda part: part[0], everything)

    def step(k, so_far):
        return combine(so_far, jax.tree.map(lambda part: part[k], everything))

    return lax.fori_loop(1, lax.axis_size(axis), step, leading)


def lifted(values):
    squares = jnp.sum(values * values, axis=1, keepdims=True)
    ones = jnp.ones_like(squares)
    left = jnp.concatenate([squares, ones, -2.0 * values], axis=1)
    right = jnp.concatenate([ones, squares, values], axis=1)
    return (left, right)


def merge_logsum(earlier, later):
    top = jnp.maximum(earlier[0], later[0])
    return (top, earlier[1] * jnp.exp(earlier[0] - top) + later[1] * jnp.exp(later[0] - top))


def shards(src_feat, tgt_feat, tgt_dual, core_matrix):
    src_rows = lax.all_gather(src_feat, "tgt", axis=1, tiled=True)
    tgt_rows = lax.all_gather(tgt_feat, "src", axis=1, tiled=True)
    src_left, src_right = lifted(src_rows)
    tgt_left, tgt_right = lifted(tgt_rows)
    src_count = lax.axis_size("src")
    tgt_count = lax.axis_size("tgt")
    row_count = src_rows.shape[0]
    col_count = tgt_rows.shape[0]
    log_src = -jnp.log(jnp.float32(row_count * src_count))
    log_tgt = -jnp.log(jnp.float32(col_count * tgt_count))
    src_dual = jnp.zeros((row_count,), jnp.float32)
    for outer_step in range(OUTER):
        projected = jnp.dot(src_left, core_matrix, precision=HIGH)
        linear = jnp.dot(projected, tgt_right.T, precision=HIGH)
        row_logits = (tgt_dual[None, :] - linear) / EPSILON
        row_max = jnp.max(row_logits, axis=1)
        row_total = jnp.sum(jnp.exp(row_logits - row_max[:, None]), axis=1)
        row_max, row_total = merged((row_max, row_total), "tgt", merge_logsum)
        src_dual = EPSILON * log_src - EPSILON * (row_max + jnp.log(row_total))
        col_logits = (src_dual[:, None] - linear) / EPSILON
        col_max = jnp.max(col_logits, axis=0)
        col_exp = jnp.exp(col_logits - col_max[None, :])
        col_total = jnp.sum(col_exp, axis=0)
        piece_max, piece_total = (
            lax.all_to_all(col_max[None, :], "src", split_axis=1, concat_axis=0, tiled=True),
            lax.all_to_all(col_total[None, :], "src", split_axis=1, concat_axis=0, tiled=True),
        )
        whole_max = jnp.max(piece_max, axis=0)
        whole_total = jnp.sum(piece_total * jnp.exp(piece_max - whole_max[None, :]), axis=0)
        dual_piece = EPSILON * log_tgt - EPSILON * (whole_max + jnp.log(whole_total))
        tgt_dual = lax.all_gather(dual_piece, "src", axis=0, tiled=True)
        coupling = jnp.exp((src_dual[:, None] + tgt_dual[None, :] - linear) / EPSILON)
        weighted = jnp.dot(coupling, tgt_left, precision=HIGH)
        core_part = jnp.dot(src_right.T, weighted, precision=HIGH)
        core_matrix = -2.0 * lax.psum(core_part, ("src", "tgt"))
    return (src_dual, tgt_dual, core_matrix)


def solution(mesh):
    placed = (
        P(("pairs", "src"), "tgt"),
        P(("pairs", "tgt"), "src"),
        P(("pairs", "tgt")),
        P("pairs", None),
    )
    return jax.shard_map(
        shards,
        mesh=mesh,
        in_specs=placed,
        out_specs=(P(("pairs", "src")), P(("pairs", "tgt")), P("pairs", None)),
        check_vma=False,
    )
```

profile of v0, /device:TPU:0, one launch (start us, length us, event | category | flops | bytes accessed | tf_op | source)
XLA Modules:
  0.0 312.0 jit_solution(1951934580604606527)
XLA Ops:
  7.9 2.2 all_gather.36
  10.4 42.7 %all-gather.11.cloned.1.call-done = f32[8,4,8192]{2,1,0:T(4,128)} async-done(((f32[1,4,8192]{2,1,0:T(4,128)}), f32[8,4,8192]{2,1,0:T(4,128)}) %all-gather.11.cloned.1.call-update) | async-done | bytes 1048592 | tf_op jit(solution)/shard_map/all_gather | solution.py:38
  55.0 3.8 %fusion.10 = (f32[128]{0:T(128)S(1)}, f32[128,8192]{1,0:T(8,128)S(1)}) fusion(f32[8192]{0:T(1024)S(1)} %copy-done.3, f32[128,34]{1,0:T(8,128)S(1)} %fusion.32, f32[8192,32]{0,1:T(8,128)S(1)} %bitcast.89, f32[8192,1]{0,1:T(1,128)S(1)} %bitcast.91, f32[8192,1]{0,1:T(1,128)S(1)} %broadcast_in_dim.10), kind=kOutput, calls=%fused_computation.18 | convolution fusion | flops 431521664 | bytes 5359104 | tf_op jit(solution)/shard_map/dot_general | solution.py:50
  59.8 1.8 all-gather.6
  61.6 1.8 all-gather.5
  64.5 3.3 %all-to-all-start = ((f32[1,8,1024]{2,0,1:T(1,128)}), f32[1,8,1024]{2,0,1:T(1,128)S(1)}, u32[]{:S(2)}, u32[]{:S(2)}) async-start(f32[1,8,1024]{2,0,1:T(1,128)} %bitcast.11), calls=%async_computation | async-start | bytes 65536 | tf_op jit(solution)/shard_map/all_to_all | solution.py:61
  67.9 3.7 %exponential_reduce_fusion.2 = f32[8192]{0:T(1024)} fusion(f32[128,8192]{1,0:T(8,128)} %copy-done.2, f32[8192]{0:T(1024)} %fusion.11, f32[128]{0:T(128)S(1)} %multiply_subtract_fusion.3), kind=kLoop, calls=%fused_computation.14 | loop fusion | flops 4186112 | bytes 4260352 | tf_op jit(solution)/shard_map/reduce_sum | solution.py:59
  71.6 2.9 all-to-all-done
  74.6 3.3 %all-to-all-start.1 = ((f32[1,8,1024]{2,0,1:T(1,128)}), f32[1,8,1024]{2,0,1:T(1,128)S(1)}, u32[]{:S(2)}, u32[]{:S(2)}) async-start(f32[1,8,1024]{2,0,1:T(1,128)} %bitcast.12), calls=%async_computation.1 | async-start | bytes 65536 | tf_op jit(solution)/shard_map/all_to_all | solution.py:62
  77.9 6.6 %all-to-all-done.1 = f32[1,8,1024]{2,0,1:T(1,128)S(1)} async-done(((f32[1,8,1024]{2,0,1:T(1,128)}), f32[1,8,1024]{2,0,1:T(1,128)S(1)}, u32[]{:S(2)}, u32[]{:S(2)}) %all-to-all-start.1) | async-done | bytes 32800 | tf_op jit(solution)/shard_map/all_to_all | solution.py:62
  84.6 30.6 %all_gather.42 = f32[8192]{0:T(1024)S(1)} all-gather(f32[1024]{0:T(1024)S(1)} %multiply_subtract_fusion.1), channel_id=1, replica_groups=mesh['pairs'=2,'src'=8,'tgt'=2] {'src'}, dimensions={0}, use_global_device_ids=true | all-gather | bytes 36864 | tf_op jit(solution)/shard_map/all_gather | solution.py:67
  115.2 6.2 %fusion.5 = f32[128,34]{1,0:T(8,128)S(1)} fusion(f32[128,8192]{1,0:T(8,128)} %copy-done.2, f32[8192]{0:T(1024)S(1)} %all_gather.42, f32[128]{0:T(128)S(1)} %multiply_subtract_fusion.3, f32[8192,32]{0,1:T(8,128)S(1)} %get-tuple-element.27, f32[8192,1]{0,1:T(1,128)S(1)} %broadcast_in_dim.10, f32[8192,1]{0,1:T(1,128)S(1)} %bitcast.92), kind=kOutput, calls=%fused_computation.9 | convolution fusion | flops 431521792 | bytes 5359104 | tf_op jit(solution)/shard_map/dot_general | solution.py:69
  121.6 57.8 %psum.14 = f32[34,34]{1,0:T(8,128)S(1)} all-reduce(f32[34,34]{1,0:T(8,128)S(1)} %fusion.31), channel_id=1, replica_groups=mesh['pairs'=2,'src'=8,'tgt'=2] {'src','tgt'}, use_global_device_ids=true, to_apply=%region_8.0 | all-reduce | flops 1156 | bytes 9248 | tf_op jit(solution)/shard_map/psum | solution.py:71
  179.7 3.8 %fusion.12 = (f32[128]{0:T(128)S(1)}, f32[128,8192]{1,0:T(8,128)S(1)}) fusion(f32[8192]{0:T(1024)S(1)} %all_gather.42, f32[128,34]{1,0:T(8,128)S(1)} %fusion.28, f32[8192,32]{0,1:T(8,128)S(1)} %bitcast.90, f32[8192,1]{0,1:T(1,128)S(1)} %bitcast.93, f32[8192,1]{0,1:T(1,128)S(1)} %broadcast_in_dim.10), kind=kOutput, calls=%fused_computation.20 | convolution fusion | flops 431521664 | bytes 5359104 | tf_op jit(solution)/shard_map/dot_general | solution.py:50
  184.5 1.8 all-gather.8
  186.3 1.8 all-gather.7
  189.3 3.3 %all-to-all-start.2 = ((f32[1,8,1024]{2,0,1:T(1,128)}), f32[1,8,1024]{2,0,1:T(1,128)S(1)}, u32[]{:S(2)}, u32[]{:S(2)}) async-start(f32[1,8,1024]{2,0,1:T(1,128)} %bitcast.19), calls=%async_computation.2 | async-start | bytes 65536 | tf_op jit(solution)/shard_map/all_to_all | solution.py:61
  192.6 3.7 %exponential_reduce_fusion = f32[8192]{0:T(1024)} fusion(f32[128,8192]{1,0:T(8,128)} %copy-done.1, f32[8192]{0:T(1024)} %fusion.13, f32[128]{0:T(128)S(1)} %multiply_subtract_fusion.2), kind=kLoop, calls=%fused_computation.5 | loop fusion | flops 4186112 | bytes 4260352 | tf_op jit(solution)/shard_map/reduce_sum | solution.py:59
  196.4 2.9 all-to-all-done.2
  199.3 3.3 %all-to-all-start.3 = ((f32[1,8,1024]{2,0,1:T(1,128)}), f32[1,8,1024]{2,0,1:T(1,128)S(1)}, u32[]{:S(2)}, u32[]{:S(2)}) async-start(f32[1,8,1024]{2,0,1:T(1,128)} %bitcast.20), calls=%async_computation.3 | async-start | bytes 65536 | tf_op jit(solution)/shard_map/all_to_all | solution.py:62
  202.7 6.6 %all-to-all-done.3 = f32[1,8,1024]{2,0,1:T(1,128)S(1)} async-done(((f32[1,8,1024]{2,0,1:T(1,128)}), f32[1,8,1024]{2,0,1:T(1,128)S(1)}, u32[]{:S(2)}, u32[]{:S(2)}) %all-to-all-start.3) | async-done | bytes 32800 | tf_op jit(solution)/shard_map/all_to_all | solution.py:62
  209.3 30.6 %all_gather.47 = f32[8192]{0:T(1024)S(1)} all-gather(f32[1024]{0:T(1024)S(1)} %multiply_subtract_fusion), channel_id=1, replica_groups=mesh['pairs'=2,'src'=8,'tgt'=2] {'src'}, dimensions={0}, use_global_device_ids=true | all-gather | bytes 36864 | tf_op jit(solution)/shard_map/all_gather | solution.py:67
  239.9 6.2 %fusion = f32[128,34]{1,0:T(8,128)S(1)} fusion(f32[128,8192]{1,0:T(8,128)} %copy-done.1, f32[8192]{0:T(1024)S(1)} %all_gather.47, f32[128]{0:T(128)S(1)} %multiply_subtract_fusion.2, f32[8192,32]{0,1:T(8,128)S(1)} %get-tuple-element.27, f32[8192,1]{0,1:T(1,128)S(1)} %broadcast_in_dim.10, f32[8192,1]{0,1:T(1,128)S(1)} %bitcast.94), kind=kOutput, calls=%fused_computation | convolution fusion | flops 431521792 | bytes 5359104 | tf_op jit(solution)/shard_map/dot_general | solution.py:69
  246.3 57.6 %psum.15 = f32[34,34]{1,0:T(8,128)S(1)} all-reduce(f32[34,34]{1,0:T(8,128)S(1)} %fusion.30), channel_id=1, replica_groups=mesh['pairs'=2,'src'=8,'tgt'=2] {'src','tgt'}, use_global_device_ids=true, to_apply=%region_15.0 | all-reduce | flops 1156 | bytes 9248 | tf_op jit(solution)/shard_map/psum | solution.py:71
  (35 shorter events, 9.2 us)
Async XLA Ops:
  7.2 3.0 copy-start
  7.2 47.8 %copy-start.3 = (f32[8192]{0:T(1024)S(1)}, f32[8192]{0:T(1024)}, u32[]{:S(2)}) copy-start(f32[8192]{0:T(1024)} %param.6) | copy-start | bytes 98308
  7.2 46.0 %all-gather.11.cloned.1.call-start = ((), (), s32[]{:S(2)}) async-start(), calls=%async_computation.4 | async-start | bytes 1179648 | tf_op jit(solution)/shard_map/all_gather | solution.py:38
  58.8 5.8 %copy-start.2 = (f32[128,8192]{1,0:T(8,128)}, f32[128,8192]{1,0:T(8,128)S(1)}, u32[]{:S(2)}) copy-start(f32[128,8192]{1,0:T(8,128)S(1)} %get-tuple-element.38) | copy-start | bytes 12582916
  64.5 10.0 %all-to-all-start = ((f32[1,8,1024]{2,0,1:T(1,128)}), f32[1,8,1024]{2,0,1:T(1,128)S(1)}, u32[]{:S(2)}, u32[]{:S(2)}) async-start(f32[1,8,1024]{2,0,1:T(1,128)} %bitcast.11), calls=%async_computation | async-start | bytes 65536 | tf_op jit(solution)/shard_map/all_to_all | solution.py:61
  74.6 10.0 %all-to-all-start.1 = ((f32[1,8,1024]{2,0,1:T(1,128)}), f32[1,8,1024]{2,0,1:T(1,128)S(1)}, u32[]{:S(2)}, u32[]{:S(2)}) async-start(f32[1,8,1024]{2,0,1:T(1,128)} %bitcast.12), calls=%async_computation.1 | async-start | bytes 65536 | tf_op jit(solution)/shard_map/all_to_all | solution.py:62
  183.5 5.8 %copy-start.1 = (f32[128,8192]{1,0:T(8,128)}, f32[128,8192]{1,0:T(8,128)S(1)}, u32[]{:S(2)}) copy-start(f32[128,8192]{1,0:T(8,128)S(1)} %get-tuple-element.40) | copy-start | bytes 12582916
  188.1 51.8 %copy-start.4 = (f32[128]{0:T(128)}, f32[128]{0:T(128)S(1)}, u32[]{:S(2)}) copy-start(f32[128]{0:T(128)S(1)} %multiply_subtract_fusion.2) | copy-start | bytes 1540
  189.3 10.0 %all-to-all-start.2 = ((f32[1,8,1024]{2,0,1:T(1,128)}), f32[1,8,1024]{2,0,1:T(1,128)S(1)}, u32[]{:S(2)}, u32[]{:S(2)}) async-start(f32[1,8,1024]{2,0,1:T(1,128)} %bitcast.19), calls=%async_computation.2 | async-start | bytes 65536 | tf_op jit(solution)/shard_map/all_to_all | solution.py:61
  199.3 10.0 %all-to-all-start.3 = ((f32[1,8,1024]{2,0,1:T(1,128)}), f32[1,8,1024]{2,0,1:T(1,128)S(1)}, u32[]{:S(2)}, u32[]{:S(2)}) async-start(f32[1,8,1024]{2,0,1:T(1,128)} %bitcast.20), calls=%async_computation.3 | async-start | bytes 65536 | tf_op jit(solution)/shard_map/all_to_all | solution.py:62
Sparse Core Ops, SparseCore 0:
  10.1 42.9 all-gather.10
where the time goes:
time: 313 us; the launch traced here: 312 us
  blocking collectives  186 us (59%)
  waiting for transfers between devices  62.4 us (20%)
  matrix products  21 us (7%)
  between operations  14.2 us (5%)
  starting transfers between devices  13.4 us (4%)
  other arithmetic  12.7 us (4%)
    psum x2, blocking collectives, shards(): core_matrix = -2.0 * lax.psum(core_part, ('src', 'tgt'))  115 us
    all_gather x2, blocking collectives, shards(): tgt_dual = lax.all_gather(dual_piece, 'src', axis=0, tiled=True)  61.2 us
    all_gather x1, waiting for transfers between devices, shards(): tgt_rows = lax.all_gather(tgt_feat, 'src', axis=1, tiled=True)  42.7 us
    all_to_all x2, waiting for transfers between devices, shards(): lax.all_to_all(col_total[None, :], 'src', split_axis=1, concat_axis=0, ti...  13.2 us
    dot_general x2, matrix products, shards(): weighted = jnp.dot(coupling, tgt_left, precision=HIGH)  12.4 us
    dot_general x2, matrix products, shards(): linear = jnp.dot(projected, tgt_right.T, precision=HIGH)  7.61 us
    reduce_sum x2, other arithmetic, shards(): col_total = jnp.sum(col_exp, axis=0)  7.45 us
    all_gather x4, blocking collectives, merged(): everything = jax.tree.map(lambda part: lax.all_gather(part, axis), array)  7.19 us
  transfers between devices with their start and end apart: 5, of which 5 were waited for; matrix products, arithmetic and copies ran while one was open for 3% of the time, Pallas kernels for 0%

commit v1 on v0

v1 whole, which is shorter than its diff:
```python
import functools
import math

import jax
import jax.numpy as jnp
from jax import lax
from jax.experimental import pallas as pl
from jax.experimental.pallas import tpu as pltpu
from jax.sharding import PartitionSpec as P

OUTER = 2
EPSILON = 0.02
SCALE = math.log2(math.e) / EPSILON
HIGH = lax.Precision.HIGHEST
F32 = jnp.float32
BF16 = jnp.bfloat16
FEAT = 32
RANKS = FEAT + 2
PAD = 40
WIDE = 48
DEPTH = 256
LANES = 128
SHIFT = 42
GROUP = 16
CHUNK = 256
NT_DIMS = (((1,), (1,)), ((), ()))


def thirds(values):
    first = values.astype(BF16).astype(F32)
    rest = values - first
    second = rest.astype(BF16).astype(F32)
    third = (rest - second).astype(BF16).astype(F32)
    return first, second, third


def left_order(parts):
    return [parts[0], parts[0], parts[1], parts[0], parts[1], parts[2]]


def right_order(parts):
    return [parts[0], parts[1], parts[0], parts[2], parts[1], parts[0]]


def stacked(rows, count):
    width = rows[0].shape[1]
    index = lax.broadcasted_iota(jnp.int32, (count, width), 0)
    out = jnp.zeros((count, width), F32)
    for k, row in enumerate(rows):
        out = jnp.where(index == k, jnp.broadcast_to(row, (count, width)), out)
    return out


def packed(core_ref, core):
    core_ref[...] = jnp.zeros_like(core_ref)
    core_ref[: core.shape[0], : core.shape[1]] = core
    return (
        core_ref[0:GROUP]
        + pltpu.roll(core_ref[GROUP : 2 * GROUP], SHIFT, 1)
        + pltpu.roll(core_ref[2 * GROUP : 3 * GROUP], 2 * SHIFT, 1)
    )


def unpacked(block):
    pieces = [block, pltpu.roll(block, LANES - SHIFT, 1), pltpu.roll(block, LANES - 2 * SHIFT, 1)]
    whole = jnp.concatenate(pieces, axis=0)
    lane = lax.broadcasted_iota(jnp.int32, whole.shape, 1)
    return jnp.where(lane < RANKS, whole, 0.0)


def row_of(blocks):
    return jnp.concatenate([blocks[k : k + 1] for k in range(blocks.shape[0])], axis=1)


def extras(cross, fixed, ones):
    rows = left_order(thirds(cross)) + list(thirds(fixed))
    if ones:
        rows += [jnp.ones_like(fixed)] * 3
    block = stacked(rows, 16).astype(BF16)
    return jnp.concatenate([block, jnp.zeros((DEPTH - 6 * FEAT - 16, block.shape[1]), BF16)], axis=0)


def row_pass(core, scale, left, right_ref, main_ref, tail_ref, part_ref):
    proj = scale * jnp.dot(core, left, precision=HIGH, preferred_element_type=F32)
    main = jnp.concatenate(left_order(thirds(proj[:FEAT])), axis=0).astype(BF16)
    main_ref[...] = main
    tail_ref[...] = proj[FEAT:PAD]
    weights = jnp.concatenate([main, extras(proj[FEAT + 1 : FEAT + 2], proj[FEAT : FEAT + 1], True)], axis=0)
    count = right_ref.shape[0]
    size = min(CHUNK, count)
    top = total = None
    for start in range(0, count, size):
        logits = jnp.dot(right_ref[start : start + size], weights, preferred_element_type=F32)
        high = jnp.max(logits, axis=0, keepdims=True)
        if top is None:
            top = high
            total = jnp.sum(jnp.exp2(logits - top), axis=0, keepdims=True)
        else:
            new = jnp.maximum(top, high)
            total = total * jnp.exp2(top - new) + jnp.sum(jnp.exp2(logits - new), axis=0, keepdims=True)
            top = new
    part = top + jnp.log2(total)
    peers, blocks, lanes = part_ref.shape
    for k in range(blocks):
        piece = part[:, k * lanes : (k + 1) * lanes]
        for peer in range(peers):
            part_ref[peer, k : k + 1, :] = piece


def first_rows(halves, src_ref, tgt_ref, dual_ref, core_ref, left_ref, tgtl_ref, right_ref, main_ref, tail_ref, part_ref):
    peers = src_ref.shape[0]
    columns = []
    for start in range(0, peers, halves):
        columns.append(jnp.concatenate([src_ref[start + t] for t in range(halves)], axis=0))
    src = jnp.concatenate(columns, axis=1)
    squares = jnp.sum(src * src, axis=0, keepdims=True)
    left_ref[0:FEAT] = -2.0 * src
    left_ref[FEAT:PAD] = stacked([jnp.ones_like(squares), squares], PAD - FEAT)

    blocks, feats, count = tgt_ref.shape
    for k in range(blocks):
        tgtl_ref[k * feats : (k + 1) * feats] = tgt_ref[k]
    tgt = tgtl_ref[0:FEAT]
    norms = jnp.sum(tgt * tgt, axis=0, keepdims=True)
    tgtl_ref[0:FEAT] = -2.0 * tgt
    tgtl_ref[FEAT:PAD] = stacked([norms, jnp.ones_like(norms)], PAD - FEAT)
    start = pl.multiple_of(lax.axis_index("src") * count, LANES)
    dual = SCALE * dual_ref[:, pl.ds(start, count)]
    rows = right_order(thirds(norms)) + [jnp.ones_like(norms)] * 3 + list(thirds(dual))
    tail = jnp.concatenate([stacked(rows, 16), jnp.zeros((DEPTH - 6 * FEAT - 16, count), F32)], axis=0)
    right = jnp.concatenate(right_order(thirds(tgt)) + [tail], axis=0)
    right_ref[...] = right.T.astype(BF16)
    row_pass(core_ref[...], -SCALE, left_ref[...], right_ref, main_ref, tail_ref, part_ref)


def later_rows(core_ref, left_ref, right_ref, main_ref, tail_ref, part_ref):
    core = unpacked(jnp.sum(core_ref[...], axis=0))
    row_pass(core[:PAD, :PAD], 2.0 * SCALE, left_ref[...], right_ref, main_ref, tail_ref, part_ref)


def fold_dual(dual_ref, right_ref, out_ref):
    out_ref[...] = right_ref[...]
    for k in range(dual_ref.shape[0]):
        dual = jnp.broadcast_to(dual_ref[k : k + 1], (LANES, LANES)).T
        parts = thirds(dual)
        old = right_ref[k * LANES : (k + 1) * LANES, LANES:].astype(F32)
        lane = lax.broadcasted_iota(jnp.int32, old.shape, 1) - (6 * FEAT + 9 - LANES)
        for t in range(3):
            old = jnp.where(lane == t, parts[t], old)
        out_ref[k * LANES : (k + 1) * LANES, LANES:] = old.astype(BF16)


def col_pass(sizes, part_ref, main_ref, tail_ref, right_ref, left_ref, tgtl_ref, own_ref, dual_ref, out_ref, pack_ref):
    src_total, tgt_total = sizes
    parts = part_ref[...]
    top = jnp.max(parts, axis=0)
    summed = top + jnp.log2(jnp.sum(jnp.exp2(parts - top[None]), axis=0))
    src_dual = -math.log2(src_total) - summed
    own_rows = own_ref.shape[0]
    pack_ref[0 : src_dual.shape[0]] = src_dual
    own_ref[...] = pack_ref[pl.ds(lax.axis_index("src") * own_rows, own_rows)] * (1.0 / SCALE)

    tail = extras(tail_ref[1:2], tail_ref[0:1] + row_of(src_dual), False)
    weights = jnp.concatenate([main_ref[...], tail], axis=0)
    src = -0.5 * left_ref[0:FEAT]
    squares = left_ref[FEAT + 1 : FEAT + 2]
    ones = left_ref[FEAT : FEAT + 1]
    feats = thirds(src)
    norms = thirds(squares)
    factors = jnp.concatenate(
        [feats[0], stacked([norms[0], ones], GROUP), feats[1], stacked([norms[1]], GROUP)], axis=0
    ).astype(BF16)
    count = right_ref.shape[0]
    size = min(CHUNK, count)
    row = lax.broadcasted_iota(jnp.int32, (LANES, LANES), 0)
    eye = row == lax.broadcasted_iota(jnp.int32, (LANES, LANES), 1)
    core = jnp.zeros((PAD, WIDE), F32)
    peers = out_ref.shape[0]
    for start in range(0, count, size):
        logits = jnp.dot(right_ref[start : start + size], weights, preferred_element_type=F32)
        high = jnp.max(logits, axis=1, keepdims=True)
        weight = jnp.exp2(logits - high)
        coarse = weight.astype(BF16)
        fine = (weight - coarse.astype(F32)).astype(BF16)
        both = lax.dot_general(factors, coarse, NT_DIMS, preferred_element_type=F32)
        rest = lax.dot_general(factors[:WIDE], fine, NT_DIMS, preferred_element_type=F32)
        moments = both[:WIDE] + both[WIDE:] + rest
        total = moments[FEAT + 1 : FEAT + 2]
        tops = []
        for k in range(0, size, LANES):
            block = jnp.broadcast_to(high[k : k + LANES], (LANES, LANES))
            tops.append(jnp.sum(jnp.where(eye, block, 0.0), axis=0, keepdims=True))
        tops = jnp.concatenate(tops, axis=1)
        dual = -math.log2(tgt_total) - (tops + jnp.log2(total))
        for k in range(0, size, LANES):
            dual_ref[(start + k) // LANES : (start + k) // LANES + 1] = dual[:, k : k + LANES]
        moments = moments * ((1.0 / tgt_total) / total)
        core = core + lax.dot_general(
            tgtl_ref[:, start : start + size], moments, NT_DIMS, precision=HIGH, preferred_element_type=F32
        )
    block = packed(pack_ref, core)
    for peer in range(peers):
        out_ref[peer, 0:GROUP] = block
    if out_ref.shape[1] > GROUP:
        for peer in range(peers):
            out_ref[peer, GROUP:] = dual_ref[...]


def finish(halves, in_ref, dual_ref, core_ref):
    half = lax.axis_index("tgt")
    for k in range(dual_ref.shape[0]):
        dual_ref[k] = in_ref[k * halves + half, GROUP:] * (1.0 / SCALE)
    core = unpacked(jnp.sum(in_ref[:, 0:GROUP], axis=0))
    core = jnp.concatenate([core[FEAT:RANKS], core[:FEAT], jnp.zeros((LANES - RANKS, LANES), F32)], axis=0)
    lane = lax.broadcasted_iota(jnp.int32, core.shape, 1)
    moved = pltpu.roll(core, 2, 1)
    moved = jnp.where(lane == 0, pltpu.roll(core, LANES - FEAT - 1, 1), moved)
    moved = jnp.where(lane == 1, pltpu.roll(core, LANES - FEAT + 1, 1), moved)
    core_ref[...] = -2.0 * moved.T[:RANKS, :RANKS]


def call(body, outs, *args, scratch=()):
    spec = pl.BlockSpec(memory_space=pltpu.VMEM)
    return pl.pallas_call(
        body,
        out_shape=[jax.ShapeDtypeStruct(shape, dtype) for shape, dtype in outs],
        in_specs=[spec] * len(args),
        out_specs=[spec] * len(outs),
        scratch_shapes=scratch,
    )(*args)


def exchanged(blocks, axes):
    return lax.all_to_all(blocks, axes, split_axis=0, concat_axis=0, tiled=True)


def shards(src_feat, tgt_feat, tgt_dual, core_matrix):
    everyone = ("src", "tgt")
    slices, halves = lax.axis_size("src"), lax.axis_size("tgt")
    peers = slices * halves
    own = src_feat.shape[0]
    whole = tgt_feat.shape[0]
    rows, cols = own * slices, whole // slices
    sizes = (rows, whole * halves)
    row_blocks, col_blocks = rows // LANES, cols // LANES

    tgt_pieces = exchanged(tgt_feat.reshape(slices, cols, -1).transpose(0, 2, 1), "src")
    src_pieces = exchanged(jnp.broadcast_to(src_feat.T[None], (peers,) + src_feat.T.shape), everyone)
    order = core_matrix.T
    order = jnp.concatenate([order[2:], order[:2]], axis=0)
    order = jnp.concatenate([order[:, 2:], order[:, 1:2], order[:, :1]], axis=1)
    order = jnp.pad(order, ((0, PAD - RANKS), (0, PAD - RANKS)))

    passed = [((6 * FEAT, rows), BF16), ((PAD - FEAT, rows), F32), ((peers, row_blocks, LANES), F32)]
    left, tgt_left, right, main, tail, part = call(
        functools.partial(first_rows, halves),
        [((PAD, rows), F32), ((PAD, cols), F32), ((cols, DEPTH), BF16)] + passed,
        src_pieces,
        tgt_pieces,
        tgt_dual.reshape(1, whole),
        order,
    )
    for step in range(OUTER):
        last = step == OUTER - 1
        src_dual, dual, core = call(
            functools.partial(col_pass, sizes),
            [
                ((own // LANES, LANES), F32),
                ((col_blocks, LANES), F32),
                ((peers, GROUP + (col_blocks if last else 0), LANES), F32),
            ],
            exchanged(part, everyone),
            main,
            tail,
            right,
            left,
            tgt_left,
            scratch=[pltpu.VMEM((max(WIDE, row_blocks), LANES), F32)],
        )
        core = exchanged(core, everyone)
        if not last:
            (right,) = call(fold_dual, [((cols, DEPTH), BF16)], dual, right)
            main, tail, part = call(later_rows, passed, core, left, right)
    dual, core = call(
        functools.partial(finish, halves),
        [((slices, col_blocks, LANES), F32), ((RANKS, RANKS), F32)],
        core,
    )
    return src_dual.reshape(own), dual.reshape(whole), core


def solution(mesh):
    placed = (
        P(("pairs", "src"), "tgt"),
        P(("pairs", "tgt"), "src"),
        P(("pairs", "tgt")),
        P("pairs", None),
    )
    return jax.shard_map(
        shards,
        mesh=mesh,
        in_specs=placed,
        out_specs=(P(("pairs", "src")), P(("pairs", "tgt")), P("pairs", None)),
        check_vma=False,
    )
```

time: 313 us -> 96.6 us (0.31)
  blocking collectives: 186 us -> 35.2 us
  waiting for transfers between devices: 62.4 us -> 20 us
  Pallas kernels: 0 us -> 22.6 us
  matrix products: 21 us -> 0 us
  between operations: 14.2 us -> 0.67 us
  other arithmetic: 12.7 us -> 0.85 us
    psum x2 -> x0, blocking collectives: 115 us -> none  [shards(): core_matrix = -2.0 * lax.psum(core_part, ('src', 'tgt'))]
    all_gather x7 -> x0, blocking collectives: 70.6 us -> none  [the longest x2 61.2 us: shards(): tgt_dual = lax.all_gather(dual_piece, 'src', axis=0, tiled=True)]
    all_gather x1 -> x0, waiting for transfers between devices: 42.7 us -> none  [shards(): tgt_rows = lax.all_gather(tgt_feat, 'src', axis=1, tiled=True)]
    all_to_all x0 -> x3, blocking collectives: none -> 35.2 us  [exchanged(): return lax.all_to_all(blocks, axes, split_axis=0, concat_axis=0, tiled=True)]
    pallas_call x0 -> x6, Pallas kernels: none -> 22.6 us  [call(): pl.pallas_call(body, out_shape=[jax.ShapeDtypeStruct(shape, dtype) for sh...]
    dot_general x8 -> x0, matrix products: 21 us -> none  [the longest x2 12.4 us: shards(): weighted = jnp.dot(coupling, tgt_left, precision=HIGH)]
    reduce_sum x7 -> x0, other arithmetic: 9.54 us -> none  [the longest x2 7.45 us: shards(): col_total = jnp.sum(col_exp, axis=0)]
    all_to_all x4 -> x3, waiting for transfers between devices: 19 us -> 20 us  [exchanged(): return lax.all_to_all(blocks, axes, split_axis=0, concat_axis=0, tiled=True)]
  transfers between devices with their start and end apart: 5 -> 3, of which waited for: 5 -> 3; matrix products, arithmetic and copies ran while one was open for 3% -> 1% of each run, Pallas kernels for 0% -> 2%
where the time goes in v1:
time: 96.6 us; the launch traced here: 95.8 us
  blocking collectives  35.2 us (36%)
  Pallas kernels  22.6 us (23%)
  waiting for transfers between devices  20 us (21%)
  starting transfers between devices  14.3 us (15%)
  local copies, waits for them, and re-layouts  2.11 us (2%)
    all_to_all x3, blocking collectives, exchanged(): return lax.all_to_all(blocks, axes, split_axis=0, concat_axis=0, tiled=True)  35.2 us
    pallas_call x6, Pallas kernels, call(): pl.pallas_call(body, out_shape=[jax.ShapeDtypeStruct(shape, dtype) for sh...  22.6 us
    all_to_all x3, waiting for transfers between devices, exchanged(): return lax.all_to_all(blocks, axes, split_axis=0, concat_axis=0, tiled=True)  20 us
    all_to_all x3, starting transfers between devices, exchanged(): return lax.all_to_all(blocks, axes, split_axis=0, concat_axis=0, tiled=True)  14.3 us
  transfers between devices with their start and end apart: 3, of which 3 were waited for; matrix products, arithmetic and copies ran while one was open for 1% of the time, Pallas kernels for 2%

profile of v1, /device:TPU:0, one launch (start us, length us, event | category | flops | bytes accessed | tf_op | source)
XLA Modules:
  0.0 95.8 jit_solution(8209530973472756858)
XLA Ops:
  0.6 0.0 copy-start.3
  0.6 7.3 %all-to-all-start.1 = ((f32[8,4,1024]{2,1,0:T(4,128)}), f32[8,4,1024]{2,1,0:T(4,128)S(1)}, u32[]{:S(2)}, u32[]{:S(2)}) async-start(f32[8,4,1024]{2,1,0:T(4,128)} %bitcast.8), calls=%async_computation.1 | async-start | bytes 262144 | tf_op jit(solution)/shard_map/all_to_all | solution.py:234
  8.0 0.0 copy-done.3
  8.0 0.1 copy.7
  8.1 7.2 %all-to-all-done.1.tgt_ref = f32[8,4,1024]{2,1,0:T(4,128)S(1)} async-done(((f32[8,4,1024]{2,1,0:T(4,128)}), f32[8,4,1024]{2,1,0:T(4,128)S(1)}, u32[]{:S(2)}, u32[]{:S(2)}) %all-to-all-start.1) | async-done | bytes 131104 | tf_op jit(solution)/shard_map/all_to_all | solution.py:234
  15.3 0.7 broadcast_in_dim.2
  16.0 3.5 %all-to-all-start = ((f32[16,16,128]{2,1,0:T(8,128)}), f32[16,16,128]{2,1,0:T(8,128)S(1)}, u32[]{:S(2)}, u32[]{:S(2)}) async-start(f32[16,16,128]{2,1,0:T(8,128)} %broadcast_in_dim.2), calls=%async_computation | async-start | bytes 262144 | tf_op jit(solution)/shard_map/all_to_all | solution.py:234
  19.5 0.1 fusion.1
  19.6 0.1 fusion
  19.7 0.7 fusion.2.core_ref
  20.4 7.0 %all-to-all-done.src_ref = f32[16,16,128]{2,1,0:T(8,128)S(1)} async-done(((f32[16,16,128]{2,1,0:T(8,128)}), f32[16,16,128]{2,1,0:T(8,128)S(1)}, u32[]{:S(2)}, u32[]{:S(2)}) %all-to-all-start) | async-done | bytes 131104 | tf_op jit(solution)/shard_map/all_to_all | solution.py:234
  27.4 0.6 copy-done.2
  28.0 3.0 %shard_map.67 = (f32[40,1024]{1,0:T(8,128)}, f32[40,1024]{1,0:T(8,128)}, bf16[1024,256]{1,0:T(8,128)(2,1)}, bf16[192,1024]{1,0:T(8,128)(2,1)}, f32[8,1024]{1,0:T(8,128)}, /*index=5*/f32[16,8,128]{2,1,0:T(8,128)}) custom-call(f32[16,16,128]{2,1,0:T(8,128)} %copy-done.2, f32[8,4,1024]{2,1,0:T(4,128)} %copy-done.1, f32[1,8192]{1,0:T(1,128)} %bitcast.11, ...), custom_call_target="tpu_custom_call" | custom-call | tf_op jit(solution)/shard_map/pallas_call | solution.py:224
  31.0 11.0 %all_to_all.30.part_ref = f32[16,8,128]{2,1,0:T(8,128)} all-to-all(f32[16,8,128]{2,1,0:T(8,128)} %get-tuple-element.18), channel_id=1, replica_groups=mesh['pairs'=2,'src'=8,'tgt'=2] {'src','tgt'}, dimensions={0} | all-to-all | bytes 131072 | tf_op jit(solution)/shard_map/all_to_all | solution.py:234
  42.0 6.3 %shard_map.68 = (f32[1,128]{1,0:T(1,128)}, f32[8,128]{1,0:T(8,128)}, f32[16,16,128]{2,1,0:T(8,128)}) custom-call(f32[16,8,128]{2,1,0:T(8,128)} %all_to_all.30.part_ref, bf16[192,1024]{1,0:T(8,128)(2,1)} %get-tuple-element.19.main_ref, f32[8,1024]{1,0:T(8,128)} %get-tuple-element.20.tail_ref, bf16[1024,256]{1,0:T(8,128)(2,1)} %get-tuple-element.21.right_ref, ...), custom_call_target="tpu_custom_call" | custom-call | tf_op jit(solution)/shard_map/pallas_call | solution.py:224
  48.4 3.5 %all-to-all-start.3 = ((f32[16,16,128]{2,1,0:T(8,128)}), f32[16,16,128]{2,1,0:T(8,128)S(1)}, u32[]{:S(2)}, u32[]{:S(2)}) async-start(f32[16,16,128]{2,1,0:T(8,128)} %get-tuple-element.24), calls=%async_computation.3 | async-start | bytes 262144 | tf_op jit(solution)/shard_map/all_to_all | solution.py:234
  51.9 2.1 %shard_map.69.right_ref = bf16[1024,256]{1,0:T(8,128)(2,1)} custom-call(f32[8,128]{1,0:T(8,128)} %get-tuple-element.25.dual_ref, bf16[1024,256]{1,0:T(8,128)(2,1)} %get-tuple-element.21.right_ref), custom_call_target="tpu_custom_call" | custom-call | tf_op jit(solution)/shard_map/pallas_call | solution.py:224
  54.0 5.8 %all-to-all-done.3.core_ref = f32[16,16,128]{2,1,0:T(8,128)S(1)} async-done(((f32[16,16,128]{2,1,0:T(8,128)}), f32[16,16,128]{2,1,0:T(8,128)S(1)}, u32[]{:S(2)}, u32[]{:S(2)}) %all-to-all-start.3) | async-done | bytes 131104 | tf_op jit(solution)/shard_map/all_to_all | solution.py:234
  59.7 0.7 copy-done
  60.4 3.1 %shard_map.70 = (bf16[192,1024]{1,0:T(8,128)(2,1)}, f32[8,1024]{1,0:T(8,128)}, f32[16,8,128]{2,1,0:T(8,128)}) custom-call(f32[16,16,128]{2,1,0:T(8,128)} %copy-done, f32[40,1024]{1,0:T(8,128)} %get-tuple-element.22.left_ref, bf16[1024,256]{1,0:T(8,128)(2,1)} %shard_map.69.right_ref), custom_call_target="tpu_custom_call" | custom-call | tf_op jit(solution)/shard_map/pallas_call | solution.py:224
  63.5 11.0 %all_to_all.31.part_ref = f32[16,8,128]{2,1,0:T(8,128)} all-to-all(f32[16,8,128]{2,1,0:T(8,128)} %get-tuple-element.26), channel_id=1, replica_groups=mesh['pairs'=2,'src'=8,'tgt'=2] {'src','tgt'}, dimensions={0} | all-to-all | bytes 131072 | tf_op jit(solution)/shard_map/all_to_all | solution.py:234
  74.6 6.3 %shard_map.71 = (f32[1,128]{1,0:T(1,128)}, f32[8,128]{1,0:T(8,128)}, f32[16,24,128]{2,1,0:T(8,128)}) custom-call(f32[16,8,128]{2,1,0:T(8,128)} %all_to_all.31.part_ref, bf16[192,1024]{1,0:T(8,128)(2,1)} %get-tuple-element.27.main_ref, f32[8,1024]{1,0:T(8,128)} %get-tuple-element.28.tail_ref, bf16[1024,256]{1,0:T(8,128)(2,1)} %shard_map.69.right_ref, ...), custom_call_target="tpu_custom_call" | custom-call | tf_op jit(solution)/shard_map/pallas_call | solution.py:224
  80.9 13.1 %all_to_all.32.in_ref = f32[16,24,128]{2,1,0:T(8,128)} all-to-all(f32[16,24,128]{2,1,0:T(8,128)} %get-tuple-element.30), channel_id=1, replica_groups=mesh['pairs'=2,'src'=8,'tgt'=2] {'src','tgt'}, dimensions={0} | all-to-all | bytes 393216 | tf_op jit(solution)/shard_map/all_to_all | solution.py:234
  94.0 1.8 %shard_map.72 = (f32[8,8,128]{2,1,0:T(8,128)}, f32[34,34]{1,0:T(8,128)}) custom-call(f32[16,24,128]{2,1,0:T(8,128)} %all_to_all.32.in_ref), custom_call_target="tpu_custom_call" | custom-call | tf_op jit(solution)/shard_map/pallas_call | solution.py:224
  (8 shorter events, 0.0 us)
Async XLA Ops:
  0.6 7.3 %copy-start.3 = (f32[34,34]{1,0:T(8,128)S(1)}, f32[34,34]{1,0:T(8,128)}, u32[]{:S(2)}) copy-start(f32[34,34]{1,0:T(8,128)} %param.7) | copy-start | bytes 13876
  0.6 14.7 %all-to-all-start.1 = ((f32[8,4,1024]{2,1,0:T(4,128)}), f32[8,4,1024]{2,1,0:T(4,128)S(1)}, u32[]{:S(2)}, u32[]{:S(2)}) async-start(f32[8,4,1024]{2,1,0:T(4,128)} %bitcast.8), calls=%async_computation.1 | async-start | bytes 262144 | tf_op jit(solution)/shard_map/all_to_all | solution.py:234
  8.1 7.2 %copy-start.4 = (f32[128,16]{0,1:T(8,128)S(1)}, f32[128,16]{0,1:T(8,128)}, u32[]{:S(2)}) copy-start(f32[128,16]{0,1:T(8,128)} %param.4) | copy-start | bytes 24580
  15.3 0.7 copy-start.1
  16.0 11.4 %all-to-all-start = ((f32[16,16,128]{2,1,0:T(8,128)}), f32[16,16,128]{2,1,0:T(8,128)S(1)}, u32[]{:S(2)}, u32[]{:S(2)}) async-start(f32[16,16,128]{2,1,0:T(8,128)} %broadcast_in_dim.2), calls=%async_computation | async-start | bytes 262144 | tf_op jit(solution)/shard_map/all_to_all | solution.py:234
  27.4 0.7 copy-start.2
  48.4 11.4 %all-to-all-start.3 = ((f32[16,16,128]{2,1,0:T(8,128)}), f32[16,16,128]{2,1,0:T(8,128)S(1)}, u32[]{:S(2)}, u32[]{:S(2)}) async-start(f32[16,16,128]{2,1,0:T(8,128)} %get-tuple-element.24), calls=%async_computation.3 | async-start | bytes 262144 | tf_op jit(solution)/shard_map/all_to_all | solution.py:234
  59.7 0.7 copy-start

commit v2 on v1

--- a/solution.py
+++ b/solution.py
@@ -23,6 +23,7 @@
 SHIFT = 42
 GROUP = 16
 CHUNK = 256
+VMEM_LIMIT = 20 << 20
 NT_DIMS = (((1,), (1,)), ((), ()))
 
 
@@ -107,19 +108,34 @@
             part_ref[peer, k : k + 1, :] = piece
 
 
-def first_rows(halves, src_ref, tgt_ref, dual_ref, core_ref, left_ref, tgtl_ref, right_ref, main_ref, tail_ref, part_ref):
-    peers = src_ref.shape[0]
+def first_rows(halves, *refs):
+    src_refs, refs = refs[:halves], refs[halves:]
+    dual_ref, core_ref, left_ref, tgtl_ref, right_ref, main_ref, tail_ref, part_ref = refs
+    feats = FEAT // halves
+    mine = lax.axis_index("tgt")
     columns = []
-    for start in range(0, peers, halves):
-        columns.append(jnp.concatenate([src_ref[start + t] for t in range(halves)], axis=0))
+    for k in range(src_refs[0].shape[0]):
+        pieces = [ref[k, :feats] for ref in src_refs]
+        slots = []
+        for t in range(halves):
+            slot = pieces[0]
+            for shift in range(1, halves):
+                slot = jnp.where(lax.rem(t + shift, halves) == mine, pieces[shift], slot)
+            slots.append(slot)
+        columns.append(jnp.concatenate(slots, axis=0))
     src = jnp.concatenate(columns, axis=1)
     squares = jnp.sum(src * src, axis=0, keepdims=True)
     left_ref[0:FEAT] = -2.0 * src
     left_ref[FEAT:PAD] = stacked([jnp.ones_like(squares), squares], PAD - FEAT)
 
-    blocks, feats, count = tgt_ref.shape
+    all_ref = src_refs[0]
+    blocks = all_ref.shape[0]
+    depth = FEAT // blocks
+    count = tgtl_ref.shape[1]
     for k in range(blocks):
-        tgtl_ref[k * feats : (k + 1) * feats] = tgt_ref[k]
+        for j in range(count // LANES):
+            piece = all_ref[k, feats + j * depth : feats + (j + 1) * depth]
+            tgtl_ref[k * depth : (k + 1) * depth, j * LANES : (j + 1) * LANES] = piece
     tgt = tgtl_ref[0:FEAT]
     norms = jnp.sum(tgt * tgt, axis=0, keepdims=True)
     tgtl_ref[0:FEAT] = -2.0 * tgt
@@ -227,6 +243,7 @@
         in_specs=[spec] * len(args),
         out_specs=[spec] * len(outs),
         scratch_shapes=scratch,
+        compiler_params=pltpu.CompilerParams(vmem_limit_bytes=VMEM_LIMIT),
     )(*args)
 
 
@@ -244,8 +261,14 @@
     sizes = (rows, whole * halves)
     row_blocks, col_blocks = rows // LANES, cols // LANES
 
-    tgt_pieces = exchanged(tgt_feat.reshape(slices, cols, -1).transpose(0, 2, 1), "src")
-    src_pieces = exchanged(jnp.broadcast_to(src_feat.T[None], (peers,) + src_feat.T.shape), everyone)
+    feats = src_feat.shape[1]
+    tgt_pieces = tgt_feat.reshape(slices, col_blocks, LANES, -1).transpose(0, 1, 3, 2).reshape(slices, -1, LANES)
+    src_pieces = jnp.broadcast_to(src_feat.T[None], (slices, feats, own))
+    pieces = exchanged(jnp.concatenate([src_pieces, tgt_pieces], axis=1), "src")
+    others = []
+    for shift in range(1, halves):
+        ring = [(k, (k + shift) % halves) for k in range(halves)]
+        others.append(lax.ppermute(pieces[:, :feats], "tgt", ring))
     order = core_matrix.T
     order = jnp.concatenate([order[2:], order[:2]], axis=0)
     order = jnp.concatenate([order[:, 2:], order[:, 1:2], order[:, :1]], axis=1)
@@ -255,8 +278,8 @@
     left, tgt_left, right, main, tail, part = call(
         functools.partial(first_rows, halves),
         [((PAD, rows), F32), ((PAD, cols), F32), ((cols, DEPTH), BF16)] + passed,
-        src_pieces,
-        tgt_pieces,
+        pieces,
+        *others,
         tgt_dual.reshape(1, whole),
         order,
     )

time: 96.6 us -> 75.9 us (0.79)
  Pallas kernels: 22.6 us -> 13.6 us
  blocking collectives: 35.2 us -> 31 us
  waiting for transfers between devices: 20 us -> 16.5 us
  starting transfers between devices: 14.3 us -> 11 us
  local copies, waits for them, and re-layouts: 2.11 us -> 0.82 us
  other arithmetic: 0.85 us -> 1.83 us
    pallas_call x6, Pallas kernels: 22.6 us -> 13.6 us  [call(): pl.pallas_call(body, out_shape=[jax.ShapeDtypeStruct(shape, dtype) for sh...]
    all_to_all x3 -> x2, waiting for transfers between devices: 20 us -> 15.3 us  [exchanged(): return lax.all_to_all(blocks, axes, split_axis=0, concat_axis=0, tiled=True)]
    all_to_all x3, blocking collectives: 35.2 us -> 31 us  [exchanged(): return lax.all_to_all(blocks, axes, split_axis=0, concat_axis=0, tiled=True)]
    all_to_all x3 -> x2, starting transfers between devices: 14.3 us -> 11 us  [exchanged(): return lax.all_to_all(blocks, axes, split_axis=0, concat_axis=0, tiled=True)]
    concatenate x0 -> x1, other arithmetic: none -> 1.6 us  [shards(): pieces = exchanged(jnp.concatenate([src_pieces, tgt_pieces], axis=1), 'src')]
    unnamed x11 -> x5, local copies, waits for them, and re-layouts: 1.41 us -> 0.1 us
    ppermute x0 -> x1, waiting for transfers between devices: none -> 1.15 us  [shards(): others.append(lax.ppermute(pieces[:, :feats], 'tgt', ring))]
  transfers between devices with their start and end apart: 3 -> 3, of which waited for: 3 -> 3; matrix products, arithmetic and copies ran while one was open for 1% -> 0% of each run, Pallas kernels for 2% -> 0%
where the time goes in v2:
time: 75.9 us; the launch traced here: 75.4 us
  blocking collectives  31 us (41%)
  waiting for transfers between devices  16.5 us (22%)
  Pallas kernels  13.6 us (18%)
  starting transfers between devices  11 us (14%)
  other arithmetic  1.83 us (2%)
  local copies, waits for them, and re-layouts  0.82 us (1%)
    all_to_all x3, blocking collectives, exchanged(): return lax.all_to_all(blocks, axes, split_axis=0, concat_axis=0, tiled=True)  31 us
    all_to_all x2, waiting for transfers between devices, exchanged(): return lax.all_to_all(blocks, axes, split_axis=0, concat_axis=0, tiled=True)  15.3 us
    pallas_call x6, Pallas kernels, call(): pl.pallas_call(body, out_shape=[jax.ShapeDtypeStruct(shape, dtype) for sh...  13.6 us
    all_to_all x2, starting transfers between devices, exchanged(): return lax.all_to_all(blocks, axes, split_axis=0, concat_axis=0, tiled=True)  11 us
    concatenate x1, other arithmetic, shards(): pieces = exchanged(jnp.concatenate([src_pieces, tgt_pieces], axis=1), 'src')  1.6 us
  transfers between devices with their start and end apart: 3, of which 3 were waited for; matrix products, arithmetic and copies ran while one was open for 0% of the time, Pallas kernels for 0%

profile of v2, /device:TPU:0, one launch (start us, length us, event | category | flops | bytes accessed | tf_op | source)
XLA Modules:
  0.0 75.4 jit_solution(13468909747498479421)
XLA Ops:
  0.6 0.7 broadcast_in_dim.2
  1.3 1.6 %pad_maximum_fusion = f32[8,48,128]{2,1,0:T(8,128)} fusion(f32[8,32,128]{2,1,0:T(8,128)} %bitcast.11, f32[8,16,128]{2,1,0:T(8,128)S(1)} %broadcast_in_dim.2), kind=kLoop, calls=%fused_computation | loop fusion | flops 49152 | bytes 393216 | tf_op jit(solution)/shard_map/concatenate | solution.py:267
  2.9 0.0 copy-start.1
  2.9 7.4 %all-to-all-start = ((f32[8,48,128]{2,1,0:T(8,128)}), f32[8,48,128]{2,1,0:T(8,128)S(1)}, u32[]{:S(2)}, u32[]{:S(2)}) async-start(f32[8,48,128]{2,1,0:T(8,128)} %pad_maximum_fusion), calls=%async_computation | async-start | bytes 393216 | tf_op jit(solution)/shard_map/all_to_all | solution.py:251
  10.4 0.0 copy-done.1
  10.4 0.1 copy.8
  10.5 0.1 fusion.1
  10.6 0.1 fusion
  10.6 7.7 %all-to-all-done.refs_0_ = f32[8,48,128]{2,1,0:T(8,128)S(1)} async-done(((f32[8,48,128]{2,1,0:T(8,128)}), f32[8,48,128]{2,1,0:T(8,128)S(1)}, u32[]{:S(2)}, u32[]{:S(2)}) %all-to-all-start) | async-done | bytes 196640 | tf_op jit(solution)/shard_map/all_to_all | solution.py:251
  18.3 0.1 collective-permute-start
  18.4 0.1 fusion.2.refs_3_
  18.5 1.2 %collective-permute-done.refs_1_ = f32[8,16,128]{2,1,0:T(8,128)S(1)} collective-permute-done((f32[8,16,128]{2,1,0:T(8,128)S(1)}, f32[8,16,128]{2,1,0:T(8,128)S(1)}, u32[]{:S(2)}, u32[]{:S(2)}) %collective-permute-start) | collective-permute-done | bytes 65568 | tf_op jit(solution)/shard_map/ppermute | solution.py:271
  19.7 0.0 copy-done
  19.7 1.4 %shard_map.67 = (f32[40,1024]{1,0:T(8,128)S(1)}, f32[40,1024]{1,0:T(8,128)S(1)}, bf16[1024,256]{1,0:T(8,128)(2,1)S(1)}, bf16[192,1024]{1,0:T(8,128)(2,1)S(1)}, f...) custom-call(f32[8,48,128]{2,1,0:T(8,128)S(1)} %all-to-all-done.refs_0_, f32[8,16,128]{2,1,0:T(8,128)S(1)} %collective-permute-done.refs_1_, ...), custom_call_target="tpu_custom_call" | custom-call | tf_op jit(solution)/shard_map/pallas_call | solution.py:240
  21.1 10.0 %all_to_all.25.part_ref = f32[16,8,128]{2,1,0:T(8,128)S(1)} all-to-all(f32[16,8,128]{2,1,0:T(8,128)S(1)} %get-tuple-element.18), channel_id=1, replica_groups=mesh['pairs'=2,'src'=8,'tgt'=2] {'src','tgt'}, dimensions={0} | all-to-all | bytes 131072 | tf_op jit(solution)/shard_map/all_to_all | solution.py:251
  31.0 5.0 %shard_map.68 = (f32[1,128]{1,0:T(1,128)}, f32[8,128]{1,0:T(8,128)S(1)}, f32[16,16,128]{2,1,0:T(8,128)}) custom-call(f32[16,8,128]{2,1,0:T(8,128)S(1)} %all_to_all.25.part_ref, bf16[192,1024]{1,0:T(8,128)(2,1)S(1)} %get-tuple-element.19.main_ref, f32[8,1024]{1,0:T(8,128)S(1)} %get-tuple-element.20.tail_ref, ...), custom_call_target="tpu_custom_call" | custom-call | tf_op jit(solution)/shard_map/pallas_call | solution.py:240
  36.1 3.5 %all-to-all-start.2 = ((f32[16,16,128]{2,1,0:T(8,128)}), f32[16,16,128]{2,1,0:T(8,128)S(1)}, u32[]{:S(2)}, u32[]{:S(2)}) async-start(f32[16,16,128]{2,1,0:T(8,128)} %get-tuple-element.24), calls=%async_computation.2 | async-start | bytes 262144 | tf_op jit(solution)/shard_map/all_to_all | solution.py:251
  39.6 0.2 shard_map.69.right_ref
  39.8 7.6 %all-to-all-done.2.core_ref = f32[16,16,128]{2,1,0:T(8,128)S(1)} async-done(((f32[16,16,128]{2,1,0:T(8,128)}), f32[16,16,128]{2,1,0:T(8,128)S(1)}, u32[]{:S(2)}, u32[]{:S(2)}) %all-to-all-start.2) | async-done | bytes 131104 | tf_op jit(solution)/shard_map/all_to_all | solution.py:251
  47.4 1.3 %shard_map.70 = (bf16[192,1024]{1,0:T(8,128)(2,1)S(1)}, f32[8,1024]{1,0:T(8,128)S(1)}, f32[16,8,128]{2,1,0:T(8,128)S(1)}) custom-call(f32[16,16,128]{2,1,0:T(8,128)S(1)} %all-to-all-done.2.core_ref, f32[40,1024]{1,0:T(8,128)S(1)} %get-tuple-element.22.left_ref, bf16[1024,256]{1,0:T(8,128)(2,1)S(1)} %shard_map.69.right_ref), custom_call_target="tpu_custom_call" | custom-call | tf_op jit(solution)/shard_map/pallas_call | solution.py:240
  48.8 9.5 %all_to_all.26.part_ref = f32[16,8,128]{2,1,0:T(8,128)S(1)} all-to-all(f32[16,8,128]{2,1,0:T(8,128)S(1)} %get-tuple-element.26), channel_id=1, replica_groups=mesh['pairs'=2,'src'=8,'tgt'=2] {'src','tgt'}, dimensions={0} | all-to-all | bytes 131072 | tf_op jit(solution)/shard_map/all_to_all | solution.py:251
  58.3 4.7 %shard_map.71 = (f32[1,128]{1,0:T(1,128)}, f32[8,128]{1,0:T(8,128)}, f32[16,24,128]{2,1,0:T(8,128)S(1)}) custom-call(f32[16,8,128]{2,1,0:T(8,128)S(1)} %all_to_all.26.part_ref, bf16[192,1024]{1,0:T(8,128)(2,1)S(1)} %get-tuple-element.27.main_ref, f32[8,1024]{1,0:T(8,128)S(1)} %get-tuple-element.28.tail_ref, bf16[1024,256]{1,0:T(8,128)(2,1)S(1)} %shard_map.69.right_ref, ...), custom_call_target="tpu_custom_call" | custom-call | tf_op jit(solution)/shard_map/pallas_call | solution.py:240
  63.0 11.5 %all_to_all.27.in_ref = f32[16,24,128]{2,1,0:T(8,128)S(1)} all-to-all(f32[16,24,128]{2,1,0:T(8,128)S(1)} %get-tuple-element.30), channel_id=1, replica_groups=mesh['pairs'=2,'src'=8,'tgt'=2] {'src','tgt'}, dimensions={0} | all-to-all | bytes 393216 | tf_op jit(solution)/shard_map/all_to_all | solution.py:251
  74.5 0.8 %shard_map.72 = (f32[8,8,128]{2,1,0:T(8,128)}, f32[34,34]{1,0:T(8,128)}) custom-call(f32[16,24,128]{2,1,0:T(8,128)S(1)} %all_to_all.27.in_ref), custom_call_target="tpu_custom_call" | custom-call | tf_op jit(solution)/shard_map/pallas_call | solution.py:240
  (4 shorter events, 0.0 us)
Async XLA Ops:
  2.9 7.4 %copy-start.1 = (f32[34,34]{1,0:T(8,128)S(1)}, f32[34,34]{1,0:T(8,128)}, u32[]{:S(2)}) copy-start(f32[34,34]{1,0:T(8,128)} %param.7) | copy-start | bytes 13876
  2.9 15.4 %all-to-all-start = ((f32[8,48,128]{2,1,0:T(8,128)}), f32[8,48,128]{2,1,0:T(8,128)S(1)}, u32[]{:S(2)}, u32[]{:S(2)}) async-start(f32[8,48,128]{2,1,0:T(8,128)} %pad_maximum_fusion), calls=%async_computation | async-start | bytes 393216 | tf_op jit(solution)/shard_map/all_to_all | solution.py:251
  18.3 1.3 %copy-start = (f32[8192]{0:T(1024)S(1)}, f32[8192]{0:T(1024)}, u32[]{:S(2)}) copy-start(f32[8192]{0:T(1024)} %param.6) | copy-start | bytes 98308
  18.3 1.3 %collective-permute-start = (f32[8,16,128]{2,1,0:T(8,128)S(1)}, f32[8,16,128]{2,1,0:T(8,128)S(1)}, u32[]{:S(2)}, u32[]{:S(2)}) collective-permute-start(f32[8,16,128]{2,1,0:T(8,128)S(1)} %slice.24), channel_id=1, source_target_pairs={{0,1},{1,0},{2,3},{3,2},{4,5},{5,4},{6,7},{7,6},{8,9},{9,8},{10,11... | collective-permute-start | bytes 196616 | tf_op jit(solution)/shard_map/ppermute | solution.py:271
  36.1 11.4 %all-to-all-start.2 = ((f32[16,16,128]{2,1,0:T(8,128)}), f32[16,16,128]{2,1,0:T(8,128)S(1)}, u32[]{:S(2)}, u32[]{:S(2)}) async-start(f32[16,16,128]{2,1,0:T(8,128)} %get-tuple-element.24), calls=%async_computation.2 | async-start | bytes 262144 | tf_op jit(solution)/shard_map/all_to_all | solution.py:251
